TPU v7x, 32 devices: a whole 2x2x4 slice. The times are simulated.
32 devices in a mesh: dp: 8 (over z, x), seq: 4 (over y, core).
Axes of the slice: x: 2, y: 2, z: 4, core: 2. Of those that a mesh axis runs over, the one named last changes fastest.
Arguments:
- spatial_qkv: bfloat16 [8, 3, 4, 128, 1152], P('dp', None, 'seq'), may hold values from -24 to 24
- temporal_qkv: bfloat16 [8, 3, 4, 128, 1152], P('dp', None, 'seq'), may hold values from -24 to 24
- cotangent: bfloat16 [8, 4, 128, 1152], P('dp', 'seq'), may hold values from -6 to 6
- spatial_gate: float32 [8, 1152], P('dp'), may hold values from -4 to 4
- temporal_gate: float32 [8, 1152], P('dp'), may hold values from -4 to 4
- temporal_proj: bfloat16 [1152, 1152], replicated, may hold values from -0.1875 to 0.1875
- live_counts: int32 [8, 2], P('dp'), may hold values from 2 to 128, as said below
Outputs:
- temporal_qkv_grad: bfloat16 [8, 3, 4, 128, 1152], P('dp', None, 'seq')
- spatial_proj_grad: float32 [1152, 1152], P('seq', 'dp')
- temporal_proj_grad: float32 [1152, 1152], P('seq', 'dp')
Inputs may be any that keep to these rules, and one draw needn't show every extreme that they name: live_counts[g, 0] counts a clip's live frames, at most 4; live_counts[g, 1] counts the live positions of each of its frames, at most 128; in every draw some clip has all 4 frames and all 128 positions live.
All inputs are finite; a program needn't handle non-finite values.
Results may differ from a plain program's by a relative error of at most 0.015.
Values may be sent and summed in bfloat16 or wider, within the bound.
A program may use at most 64 MiB of HBM per device.

v0:
```python
import jax
import jax.numpy as jnp
from jax import lax
from jax.sharding import PartitionSpec as P

HEADS = 16
HD = 72


def attend(queries, key_block, value_block, key_keep, score_form, mix_form):
    head_split = queries.shape[:-1] + (HEADS, HD)
    q_heads = queries.reshape(head_split)
    k_heads = key_block.reshape(head_split)
    v_heads = value_block.reshape(head_split)
    scores = jnp.einsum(score_form, q_heads, k_heads, preferred_element_type=jnp.float32) * HD ** (
        -0.5
    )
    scores = jnp.where(key_keep[:, None, None, :], scores, -1e30)
    shifted = scores - jnp.max(scores, axis=-1, keepdims=True)
    expo = jnp.exp(shifted)
    attention_weights = (expo / jnp.sum(expo, axis=-1, keepdims=True)).astype(jnp.bfloat16)
    mixed = jnp.einsum(mix_form, attention_weights, v_heads, preferred_element_type=jnp.float32)
    return mixed.reshape(queries.shape)


def body(
    spatial_qkv, temporal_qkv, cotangent, spatial_gate, temporal_gate, temporal_proj, live_counts
):
    spatial = spatial_qkv[0]
    temporal = temporal_qkv[0]
    incoming = cotangent[0]
    frame_count, position_count, width = incoming.shape
    group_size = lax.axis_size("seq")
    member = lax.axis_index("seq")
    live_frames = live_counts[0, 0]
    live_positions = live_counts[0, 1]
    frame_ids = member * frame_count + jnp.arange(frame_count, dtype=jnp.int32)
    position_ids = jnp.arange(position_count, dtype=jnp.int32)
    token_mask = (
        (frame_ids[:, None] < live_frames) & (position_ids[None, :] < live_positions)
    ).astype(jnp.float32)
    flowing = token_mask[:, :, None] * incoming.astype(jnp.float32)
    temporal_error = (flowing * temporal_gate[0]).astype(jnp.bfloat16)
    temporal_back = lax.dot_general(
        temporal_error, temporal_proj, (((2,), (1,)), ((), ())), preferred_element_type=jnp.float32
    ).astype(jnp.bfloat16)
    stacked = jnp.concatenate([temporal, temporal_back[None]], axis=0)
    exchanged = lax.all_to_all(stacked, "seq", split_axis=2, concat_axis=1, tiled=True)
    spatial_keep = position_ids[None, :] < live_positions
    spatial_out = attend(
        spatial[0], spatial[1], spatial[2], spatial_keep, "bqhd,bkhd->bhqk", "bhqk,bkhd->bqhd"
    ).astype(jnp.bfloat16)
    total_frames = exchanged.shape[1]
    slice_positions = exchanged.shape[2]
    temporal_keep = jnp.broadcast_to(
        jnp.arange(total_frames, dtype=jnp.int32)[None, :] < live_frames,
        (slice_positions, total_frames),
    )

    def temporal_attend(queries, key_block, value_block):
        return attend(
            queries, key_block, value_block, temporal_keep, "qbhd,kbhd->bhqk", "bhqk,kbhd->qbhd"
        )

    temporal_result, pullback = jax.vjp(temporal_attend, exchanged[0], exchanged[1], exchanged[2])
    temporal_out = temporal_result.astype(jnp.bfloat16)
    input_grads = jnp.stack(pullback(exchanged[3].astype(jnp.float32)))
    temporal_frames = lax.all_to_all(temporal_out, "seq", split_axis=0, concat_axis=1, tiled=True)
    grads_home = lax.all_to_all(input_grads, "seq", split_axis=1, concat_axis=2, tiled=True)
    tokens = frame_count * position_count
    flat_spatial = spatial_out.reshape(tokens, width)
    flat_temporal = temporal_frames.reshape(tokens, width)
    slice_width = width // group_size
    column_spatial, column_temporal = (
        lax.all_to_all(flat_spatial, "seq", split_axis=1, concat_axis=0, tiled=True),
        lax.all_to_all(flat_temporal, "seq", split_axis=1, concat_axis=0, tiled=True),
    )
    spatial_scale = spatial_gate[0]
    temporal_scale = temporal_gate[0]
    starting = jnp.zeros((slice_width, 2, width), jnp.float32)
    cot_piece = lax.all_gather(incoming.reshape(tokens, width), "seq", axis=0, tiled=True)
    shards = cot_piece.shape[0] // tokens

    def one_block(block, total):
        offset = (block * tokens).astype(jnp.int32)
        rows = lax.dynamic_slice_in_dim(cot_piece, offset, tokens, 0)
        token_index = offset + jnp.arange(tokens, dtype=jnp.int32)
        frame_of = token_index // position_count
        position_of = token_index % position_count
        row_keep = ((frame_of < live_frames) & (position_of < live_positions)).astype(jnp.float32)
        masked_rows = row_keep[:, None] * rows.astype(jnp.float32)
        error_first = (masked_rows * spatial_scale).astype(jnp.bfloat16)
        error_second = (masked_rows * temporal_scale).astype(jnp.bfloat16)
        cols_first = lax.dynamic_slice_in_dim(column_spatial, offset, tokens, 0)
        cols_second = lax.dynamic_slice_in_dim(column_temporal, offset, tokens, 0)
        part_first = lax.dot_general(
            cols_first, error_first, (((0,), (0,)), ((), ())), preferred_element_type=jnp.float32
        )
        part_second = lax.dot_general(
            cols_second, error_second, (((0,), (0,)), ((), ())), preferred_element_type=jnp.float32
        )
        part_first = part_first.astype(jnp.bfloat16).astype(jnp.float32)
        part_second = part_second.astype(jnp.bfloat16).astype(jnp.float32)
        return total + jnp.stack([part_first, part_second], axis=1)

    partial_sum = lax.fori_loop(0, shards, one_block, starting)
    summed = lax.psum_scatter(partial_sum, "dp", scatter_dimension=2, tiled=True)
    return (grads_home[None], summed[:, 0], summed[:, 1])


def solution(mesh):
    return jax.shard_map(
        body,
        mesh=mesh,
        in_specs=(
            P("dp", None, "seq", None, None),
            P("dp", None, "seq", None, None),
            P("dp", "seq", None, None),
            P("dp", None),
            P("dp", None),
            P(),
            P("dp", None),
        ),
        out_specs=(P("dp", None, "seq", None, None), P("seq", "dp"), P("seq", "dp")),
        check_vma=False,
    )
```

profile of v0, /device:TPU:0, one launch (start us, length us, event | category | flops | bytes accessed | tf_op | source)
XLA Modules:
  0.0 223.8 jit_solution(1551317566120722395)
XLA Ops:
  7.9 1.6 fusion.49
  11.5 1.9 fusion.13
  13.9 0.8 copy.149
  14.6 2.2 pad_maximum_fusion
  16.9 4.3 %all-to-all-start = ((bf16[4,1,128,1152]{3,0,1,2:T(4,128)(2,1)}), bf16[4,1,128,1152]{3,0,1,2:T(4,128)(2,1)}, u32[]{:S(2)}, u32[]{:S(2)}) async-start(bf16[4,1,128,1152]{3,0,1,2:T(4,128)(2,1)} %pad_maximum_fusion), calls=%async_computation | async-start | bytes 2359296 | tf_op jit(solution)/shard_map/all_to_all | solution.py:48
  21.2 1.2 fusion.48
  22.4 0.9 copy.103
  23.3 0.9 copy.102
  24.2 0.9 copy.104
  25.7 2.2 fusion.51
  27.9 1.3 fusion.17
  29.2 11.8 %all-to-all-done = bf16[4,1,128,1152]{3,0,1,2:T(4,128)(2,1)} async-done(((bf16[4,1,128,1152]{3,0,1,2:T(4,128)(2,1)}), bf16[4,1,128,1152]{3,0,1,2:T(4,128)(2,1)}, u32[]{:S(2)}, u32[]{:S(2)}) %all-to-all-start) | async-done | bytes 1179680 | tf_op jit(solution)/shard_map/all_to_all | solution.py:48
  41.0 9.7 %slice_reduce_fusion.2 = (bf16[128,1152]{1,0:T(8,128)(2,1)}, bf16[128,1152]{1,0:T(8,128)(2,1)S(1)}, bf16[128,1152]{1,0:T(8,128)(2,1)S(1)}, bf16[128,1152]{1,0:T(8,128)(2,1)S(1)}) fusion(bf16[4,1,128,1152]{3,0,1,2:T(4,128)(2,1)} %all-to-all-done), kind=kLoop, calls=%fused_computation.59 | loop fusion | bytes 2359296 | tf_op jit(solution)/shard_map/slice | solution.py:65
  50.7 2.7 %reshape_squeeze.6 = bf16[4,32,16,72]{3,2,1,0:T(8,128)(2,1)} reshape(bf16[128,1152]{1,0:T(8,128)(2,1)} %get-tuple-element.293) | data formatting | bytes 589824 | tf_op jit(solution)/shard_map/jvp()/reshape;squeeze | solution.py:14
  53.4 1.7 reshape_squeeze.15
  55.1 1.7 reshape_squeeze.14
  56.9 0.9 reshape.200
  57.8 2.8 %fusion.50 = (f32[32,16,4]{2,1,0:T(8,128)S(1)}, f32[32,16,4,4]{2,3,1,0:T(4,128)S(1)}) fusion(bf16[4,32,16,72]{3,2,1,0:T(8,128)(2,1)} %reshape_squeeze.15, bf16[4,32,16,72]{3,2,1,0:T(8,128)(2,1)} %reshape_squeeze.14, pred[4]{0:T(512)(128)(4,1)S(1)} %iota_compare_fusion.1), kind=kOutput, calls=%fused_computation.92 | convolution fusion | flops 1202176 | bytes 630788 | tf_op jit(solution)/shard_map/jvp(qbhd,kbhd->bhqk)/dot_general | solution.py:15
  60.6 1.0 fusion.45
  61.6 3.8 %convert_reduce_fusion = (f32[32,16,4]{2,1,0:T(8,128)}, pred[32,16,4,4]{2,3,1,0:T(4,128)(4,1)}, f32[32,16,4]{2,1,0:T(8,128)S(1)}, bf16[32,16,4,4]{2,3,1,0:T(4,128)(2,1)S(1)}) fusion(f32[32,16,4,4]{2,3,1,0:T(4,128)S(1)} %get-tuple-element.329, f32[32,16,4]{2,1,0:T(8,128)S(1)} %get-tuple-element.328, f32[32,16,4]{2,1,0:T(8,128)S(1)} %multiply_divide_fusion, ...), kind=kOutput, calls=%fused_computation.53 | convolution fusion | flops 1249280 | bytes 679936 | tf_op jit(solution)/shard_map/transpose(jvp(bhqk,kbhd->qbhd))/dot_general | solution.py:22
  65.5 2.7 %fusion.46 = (f32[32,16,4]{2,1,0:T(8,128)}, f32[32,16,4,4]{2,3,1,0:T(4,128)}, bf16[32,16,4,4]{2,3,1,0:T(4,128)(2,1)S(1)}) fusion(f32[32,16,4,4]{2,3,1,0:T(4,128)S(1)} %get-tuple-element.329, f32[32,16,4]{2,1,0:T(8,128)S(1)} %get-tuple-element.328, f32[32,16,4]{2,1,0:T(8,128)S(1)} %neg.9, f32[32,16,4]{2,1,0:T(8,128)S(1)} %fusion.45, ...), kind=kLoop, calls=%fused_computation.89 | loop fusion | flops 63488 | bytes 131072 | tf_op jit(solution)/shard_map/transpose(jvp())/reduce_sum | solution.py:19
  68.2 0.8 fusion.21
  69.1 1.2 convert_element_type.190
  70.4 3.5 %all-to-all-start.3 = ((bf16[4,32,1152]{2,1,0:T(8,128)(2,1)}), bf16[4,32,1152]{2,1,0:T(8,128)(2,1)S(1)}, u32[]{:S(2)}, u32[]{:S(2)}) async-start(bf16[4,32,1152]{2,1,0:T(8,128)(2,1)} %convert_element_type.190), calls=%async_computation.3 | async-start | bytes 589824 | tf_op jit(solution)/shard_map/all_to_all | solution.py:68
  73.8 2.7 %convolution_convert_fusion.8 = bf16[16,128,72]{1,2,0:T(8,128)(2,1)} fusion(bf16[128,16,72]{0,2,1:T(8,128)(2,1)S(1)} %bitcast.87, f32[16,128]{1,0:T(8,128)S(1)} %copy-done.14, f32[16,128,128]{1,2,0:T(8,128)} %fusion.17), kind=kOutput, calls=%fused_computation.44 | convolution fusion | flops 38684800 | bytes 1646592 | tf_op jit(solution)/shard_map/bhqk,bkhd->bqhd/dot_general | solution.py:22
  76.5 3.6 %all-to-all-done.3 = bf16[4,32,1152]{2,1,0:T(8,128)(2,1)S(1)} async-done(((bf16[4,32,1152]{2,1,0:T(8,128)(2,1)}), bf16[4,32,1152]{2,1,0:T(8,128)(2,1)S(1)}, u32[]{:S(2)}, u32[]{:S(2)}) %all-to-all-start.3) | async-done | bytes 294944 | tf_op jit(solution)/shard_map/all_to_all | solution.py:68
  80.1 0.7 copy-done.1
  80.9 3.5 %all-to-all-start.2 = ((bf16[128,4,288]{0,2,1:T(8,128)(2,1)}), bf16[128,4,288]{0,2,1:T(8,128)(2,1)S(1)}, u32[]{:S(2)}, u32[]{:S(2)}) async-start(bf16[128,4,288]{0,2,1:T(8,128)(2,1)} %bitcast.88), calls=%async_computation.2 | async-start | bytes 589824 | tf_op jit(solution)/shard_map/all_to_all | solution.py:75
  84.3 1.3 all_to_all.53
  85.7 1.0 copy.110
  86.6 4.0 %all-to-all-done.2 = bf16[128,4,288]{0,2,1:T(8,128)(2,1)S(1)} async-done(((bf16[128,4,288]{0,2,1:T(8,128)(2,1)}), bf16[128,4,288]{0,2,1:T(8,128)(2,1)S(1)}, u32[]{:S(2)}, u32[]{:S(2)}) %all-to-all-start.2) | async-done | bytes 294944 | tf_op jit(solution)/shard_map/all_to_all | solution.py:75
  90.6 4.1 %all-to-all-start.4 = ((bf16[128,4,288]{0,2,1:T(8,128)(2,1)}), bf16[128,4,288]{0,2,1:T(8,128)(2,1)}, u32[]{:S(2)}, u32[]{:S(2)}) async-start(bf16[128,4,288]{0,2,1:T(8,128)(2,1)} %copy.110), calls=%async_computation.4 | async-start | bytes 589824 | tf_op jit(solution)/shard_map/all_to_all | solution.py:76
  95.3 5.9 %all-to-all-done.4 = bf16[128,4,288]{0,2,1:T(8,128)(2,1)} async-done(((bf16[128,4,288]{0,2,1:T(8,128)(2,1)}), bf16[128,4,288]{0,2,1:T(8,128)(2,1)}, u32[]{:S(2)}, u32[]{:S(2)}) %all-to-all-start.4) | async-done | bytes 294944 | tf_op jit(solution)/shard_map/all_to_all | solution.py:76
  101.2 1.2 copy.118
  102.4 29.1 %while.16 = (s32[]{:T(128)}, f32[288,2,1152]{2,0,1:T(8,128)}, bf16[512,288]{1,0:T(8,128)(2,1)S(1)}, s32[]{:T(128)}, s32[]{:T(128)}, /*index=5*/bf16[512,1152]{1,...) while((s32[]{:T(128)}, f32[288,2,1152]{2,0,1:T(8,128)}, ...), condition=%wide.region_8.9_spmd.clone, body=%wide.region_7.8_spmd.clone.sunk | while | flops 174369792 | bytes 8787673 | solution.py:106
  102.4 1.3 and_convert_fusion.3
  103.8 1.4 fusion.68
  105.1 1.4 fusion.67
  106.5 1.9 select_add_fusion.2
  108.4 1.3 and_convert_fusion.3
  109.7 1.4 fusion.68
  111.1 1.4 fusion.67
  112.5 3.6 %select_add_fusion.2 = f32[288,2,1152]{2,0,1:T(8,128)} fusion(f32[288,2,1152]{2,0,1:T(8,128)} %get-tuple-element.403, bf16[288,1,1152]{2,0,1:T(8,128)(2,1)S(1)} %fusion.67, bf16[288,1,1152]{2,0,1:T(8,128)(2,1)S(1)} %fusion.68, pred[]{:T(512)S(6)} %compare.19), kind=kLoop, calls=%fused_computation.clone.1 | loop fusion | flops 2654208 | bytes 6635521 | tf_op jit(solution)/shard_map/while/body/eval_jaxpr/add | solution.py:104
  116.1 1.3 and_convert_fusion.3
  117.4 1.4 fusion.68
  118.8 1.4 fusion.67
  120.2 3.6 %select_add_fusion.2 = f32[288,2,1152]{2,0,1:T(8,128)} fusion(f32[288,2,1152]{2,0,1:T(8,128)} %get-tuple-element.403, bf16[288,1,1152]{2,0,1:T(8,128)(2,1)S(1)} %fusion.67, bf16[288,1,1152]{2,0,1:T(8,128)(2,1)S(1)} %fusion.68, pred[]{:T(512)S(6)} %compare.19), kind=kLoop, calls=%fused_computation.clone.1 | loop fusion | flops 2654208 | bytes 6635521 | tf_op jit(solution)/shard_map/while/body/eval_jaxpr/add | solution.py:104
  123.8 1.3 and_convert_fusion.3
  125.1 1.4 fusion.68
  126.5 1.4 fusion.67
  127.9 3.6 %select_add_fusion.2 = f32[288,2,1152]{2,0,1:T(8,128)} fusion(f32[288,2,1152]{2,0,1:T(8,128)} %get-tuple-element.403, bf16[288,1,1152]{2,0,1:T(8,128)(2,1)S(1)} %fusion.67, bf16[288,1,1152]{2,0,1:T(8,128)(2,1)S(1)} %fusion.68, pred[]{:T(512)S(6)} %compare.19), kind=kLoop, calls=%fused_computation.clone.1 | loop fusion | flops 2654208 | bytes 6635521 | tf_op jit(solution)/shard_map/while/body/eval_jaxpr/add | solution.py:104
  131.5 3.6 %copy.113 = f32[288,2,1152]{0,2,1:T(8,128)} copy(f32[288,2,1152]{2,0,1:T(8,128)} %get-tuple-element.226) | data formatting | bytes 5308416 | tf_op jit(solution)/shard_map/while | solution.py:106
  135.1 0.9 copy-done.4
  136.1 1.0 negate_divide_fusion
  137.1 2.6 %fusion.18 = bf16[4,32,16,72]{3,0,2,1:T(4,128)(2,1)S(1)} fusion(bf16[4,32,16,72]{3,2,1,0:T(8,128)(2,1)S(1)} %copy-done.7, f32[32,16,4,4]{2,3,1,0:T(4,128)} %get-tuple-element.316, pred[32,16,4,4]{2,3,1,0:T(4,128)(4,1)} %get-tuple-element.318, f32[32,16,4]{2,1,0:T(8,128)S(1)} %negate_divide_fusion, pred[4]{0:T(512)(128)(4,1)S(1)} %iota_compare_fusion.1), kind=kOutput, calls=%fused_computation.40 | convolution fusion | flops 1359872 | bytes 638980 | tf_op jit(solution)/shard_map/transpose(jvp(qbhd,kbhd->bhqk))/dot_general | solution.py:15
  140.3 2.6 %fusion.19 = bf16[4,32,16,72]{3,0,2,1:T(4,128)(2,1)S(1)} fusion(bf16[4,32,16,72]{3,2,1,0:T(8,128)(2,1)} %reshape_squeeze.14, f32[32,16,4,4]{2,3,1,0:T(4,128)} %get-tuple-element.316, pred[32,16,4,4]{2,3,1,0:T(4,128)(4,1)} %get-tuple-element.318, f32[32,16,4]{2,1,0:T(8,128)} %copy-done.11, pred[4]{0:T(512)(128)(4,1)S(1)} %iota_compare_fusion.1), kind=kOutput, calls=%fused_computation.41 | convolution fusion | flops 1359872 | bytes 638980 | tf_op jit(solution)/shard_map/transpose(jvp(qbhd,kbhd->bhqk))/dot_general | solution.py:15
  143.0 1.2 reshape.202
  144.3 1.9 fusion.20
  146.2 1.2 reshape.203
  147.5 1.2 pad_maximum_fusion.1
  148.7 15.1 %all_to_all.62 = bf16[3,4,32,1152]{3,2,0,1:T(8,128)(2,1)S(1)} all-to-all(bf16[3,4,32,1152]{3,2,0,1:T(8,128)(2,1)S(1)} %copy.100), channel_id=1, replica_groups=mesh['dp'=8,'seq'=4] {'seq'}, dimensions={1} | all-to-all | bytes 1769472 | tf_op jit(solution)/shard_map/all_to_all | solution.py:69
  163.8 1.0 copy.101
  164.8 50.3 %reduce-scatter.2.cloned.1.call-done = f32[288,2,144]{0,2,1:T(8,128)} async-done(((f32[288,2,1152]{0,2,1:T(8,128)}), f32[288,2,144]{0,2,1:T(8,128)}) %reduce-scatter.2.cloned.1.call-update) | async-done | bytes 331792 | tf_op jit(solution)/shard_map/reduce_scatter | solution.py:107
  215.1 1.8 slice_bitcast_fusion
  (55 shorter events, 4.9 us)
Async XLA Ops:
  7.2 4.3 %copy-start = (bf16[1152,1152]{1,0:T(8,128)(2,1)S(1)}, bf16[1152,1152]{1,0:T(8,128)(2,1)}, u32[]{:S(2)}) copy-start(bf16[1152,1152]{1,0:T(8,128)(2,1)} %param.14) | copy-start | bytes 7962628
  7.2 6.7 %copy-start.5 = (bf16[1,3,1,128,1152]{4,3,2,1,0:T(8,128)(2,1)S(1)}, bf16[1,3,1,128,1152]{4,3,2,1,0:T(8,128)(2,1)}, u32[]{:S(2)}) copy-start(bf16[1,3,1,128,1152]{4,3,2,1,0:T(8,128)(2,1)} %param.10) | copy-start | bytes 2654212
  7.2 95.2 %all-gather.3.cloned.1.call-start = ((), (), s32[]{:S(2)}) async-start(), calls=%async_computation.7 | async-start | bytes 1474560 | tf_op jit(solution)/shard_map/all_gather | solution.py:81
  16.9 24.1 %all-to-all-start = ((bf16[4,1,128,1152]{3,0,1,2:T(4,128)(2,1)}), bf16[4,1,128,1152]{3,0,1,2:T(4,128)(2,1)}, u32[]{:S(2)}, u32[]{:S(2)}) async-start(bf16[4,1,128,1152]{3,0,1,2:T(4,128)(2,1)} %pad_maximum_fusion), calls=%async_computation | async-start | bytes 2359296 | tf_op jit(solution)/shard_map/all_to_all | solution.py:48
  23.3 4.6 %copy-start.2 = (bf16[1,1,1,128,1152]{3,4,2,1,0:T(8,128)(2,1)S(1)}, bf16[1,1,1,128,1152]{3,4,2,1,0:T(8,128)(2,1)}, u32[]{:S(2)}) copy-start(bf16[1,1,1,128,1152]{3,4,2,1,0:T(8,128)(2,1)} %copy.103) | copy-start | bytes 884740
  24.2 3.7 %copy-start.3 = (bf16[1,1,1,128,1152]{3,4,2,1,0:T(8,128)(2,1)S(1)}, bf16[1,1,1,128,1152]{3,4,2,1,0:T(8,128)(2,1)}, u32[]{:S(2)}) copy-start(bf16[1,1,1,128,1152]{3,4,2,1,0:T(8,128)(2,1)} %copy.102) | copy-start | bytes 884740
  57.8 3.8 %copy-start.6 = (bf16[4,32,16,72]{3,2,1,0:T(8,128)(2,1)}, bf16[4,32,16,72]{3,2,1,0:T(8,128)(2,1)S(1)}, u32[]{:S(2)}) copy-start(bf16[4,32,16,72]{3,2,1,0:T(8,128)(2,1)S(1)} %reshape.200) | copy-start | bytes 884740
  57.8 3.8 %copy-start.8 = (bf16[4,32,16,72]{3,2,1,0:T(8,128)(2,1)S(1)}, bf16[4,32,16,72]{3,2,1,0:T(8,128)(2,1)}, u32[]{:S(2)}) copy-start(bf16[4,32,16,72]{3,2,1,0:T(8,128)(2,1)} %reshape_squeeze.6) | copy-start | bytes 884740
  68.2 0.9 copy-start.9
  68.2 5.6 %copy-start.10 = (bf16[1,1,1,128,1152]{3,4,2,1,0:T(8,128)(2,1)S(1)}, bf16[1,1,1,128,1152]{3,4,2,1,0:T(8,128)(2,1)}, u32[]{:S(2)}) copy-start(bf16[1,1,1,128,1152]{3,4,2,1,0:T(8,128)(2,1)} %copy.104) | copy-start | bytes 884740
  68.2 5.6 %copy-start.14 = (f32[16,128]{1,0:T(8,128)S(1)}, f32[16,128]{1,0:T(8,128)}, u32[]{:S(2)}) copy-start(f32[16,128]{1,0:T(8,128)} %fusion.51) | copy-start | bytes 24580
  70.4 9.8 %all-to-all-start.3 = ((bf16[4,32,1152]{2,1,0:T(8,128)(2,1)}), bf16[4,32,1152]{2,1,0:T(8,128)(2,1)S(1)}, u32[]{:S(2)}, u32[]{:S(2)}) async-start(bf16[4,32,1152]{2,1,0:T(8,128)(2,1)} %convert_element_type.190), calls=%async_computation.3 | async-start | bytes 589824 | tf_op jit(solution)/shard_map/all_to_all | solution.py:68
  76.5 25.8 %copy-start.12 = (f32[1,1152]{1,0:T(1,128)S(1)}, f32[1,1152]{1,0:T(1,128)}, u32[]{:S(2)}) copy-start(f32[1,1152]{1,0:T(1,128)} %param.13) | copy-start | bytes 13828
  76.5 25.8 %copy-start.13 = (f32[1,1152]{1,0:T(1,128)S(1)}, f32[1,1152]{1,0:T(1,128)}, u32[]{:S(2)}) copy-start(f32[1,1152]{1,0:T(1,128)} %param.12) | copy-start | bytes 13828
  80.1 0.7 copy-start.1
  80.9 9.8 %all-to-all-start.2 = ((bf16[128,4,288]{0,2,1:T(8,128)(2,1)}), bf16[128,4,288]{0,2,1:T(8,128)(2,1)S(1)}, u32[]{:S(2)}, u32[]{:S(2)}) async-start(bf16[128,4,288]{0,2,1:T(8,128)(2,1)} %bitcast.88), calls=%async_computation.2 | async-start | bytes 589824 | tf_op jit(solution)/shard_map/all_to_all | solution.py:75
  90.6 10.5 %all-to-all-start.4 = ((bf16[128,4,288]{0,2,1:T(8,128)(2,1)}), bf16[128,4,288]{0,2,1:T(8,128)(2,1)}, u32[]{:S(2)}, u32[]{:S(2)}) async-start(bf16[128,4,288]{0,2,1:T(8,128)(2,1)} %copy.110), calls=%async_computation.4 | async-start | bytes 589824 | tf_op jit(solution)/shard_map/all_to_all | solution.py:76
  94.8 120.4 %reduce-scatter.2.cloned.1.call-start = ((), (), s32[]{:S(2)}) async-start(), calls=%async_computation.6 | async-start | bytes 3981312 | tf_op jit(solution)/shard_map/reduce_scatter | solution.py:107
  135.1 0.9 copy-start.4
  135.1 2.0 copy-start.7
  137.1 2.7 %copy-start.11 = (f32[32,16,4]{2,1,0:T(8,128)}, f32[32,16,4]{2,1,0:T(8,128)S(1)}, u32[]{:S(2)}) copy-start(f32[32,16,4]{2,1,0:T(8,128)S(1)} %negate_divide_fusion) | copy-start | bytes 24580
Sparse Core Ops, SparseCore 0:
  9.6 23.3 all-gather.2
  135.3 79.7 reduce-scatter.1
where the time goes:
time: 225 us; the launch traced here: 224 us
  waiting for transfers between devices  76.3 us (34%)
  local copies, waits for them, and re-layouts  39.9 us (18%)
  matrix products  33.7 us (15%)
  other arithmetic  28 us (12%)
  starting transfers between devices  15.6 us (7%)
  blocking collectives  15.1 us (7%)
  between operations  15 us (7%)
    reduce_scatter x1, waiting for transfers between devices, body(): lax.psum_scatter(partial_sum, 'dp', scatter_dimension=2, tiled=True)  50.3 us
    all_to_all x1, blocking collectives, body(): lax.all_to_all(input_grads, 'seq', split_axis=1, concat_axis=2, tiled=True)  15.1 us
    add x4, other arithmetic, one_block(): return total + jnp.stack([part_first, part_second], axis=1)  12.6 us
    all_to_all x1, waiting for transfers between devices, body(): lax.all_to_all(stacked, 'seq', split_axis=2, concat_axis=1, tiled=True)  11.8 us
    slice x1, local copies, waits for them, and re-layouts, body(): exchanged[2]  9.68 us
    dot_general x4, matrix products, attend(): jnp.einsum(score_form, q_heads, k_heads, preferred_element_type=jnp.float32)  9.34 us
    dot_general x4, matrix products, attend(): jnp.einsum(mix_form, attention_weights, v_heads, preferred_element_type=j...  9.24 us
    all_to_all x1, waiting for transfers between devices, body(): lax.all_to_all(flat_temporal, 'seq', split_axis=1, concat_axis=0, tiled=T...  5.91 us
  transfers between devices with their start and end apart: 6, of which 5 were waited for; matrix products, arithmetic and copies ran while one was open for 29% of the time, Pallas kernels for 0%

commit v1 on v0

--- a/solution.py
+++ b/solution.py
@@ -5,6 +5,12 @@
 
 HEADS = 16
 HD = 72
+
+
+def stacked_exchange(x, name, split, join):
+    parts = jnp.split(x, lax.axis_size(name), axis=split)
+    received = lax.all_to_all(jnp.stack(parts), name, 0, 0)
+    return jnp.concatenate(received, axis=join)
 
 
 def attend(queries, key_block, value_block, key_keep, score_form, mix_form):
@@ -45,7 +51,7 @@
         temporal_error, temporal_proj, (((2,), (1,)), ((), ())), preferred_element_type=jnp.float32
     ).astype(jnp.bfloat16)
     stacked = jnp.concatenate([temporal, temporal_back[None]], axis=0)
-    exchanged = lax.all_to_all(stacked, "seq", split_axis=2, concat_axis=1, tiled=True)
+    exchanged = stacked_exchange(stacked, "seq", 2, 1)
     spatial_keep = position_ids[None, :] < live_positions
     spatial_out = attend(
         spatial[0], spatial[1], spatial[2], spatial_keep, "bqhd,bkhd->bhqk", "bhqk,bkhd->bqhd"

time: 225 us -> 217 us (0.964)
  local copies, waits for them, and re-layouts: 39.9 us -> 31 us
  waiting for transfers between devices: 76.3 us -> 78.8 us
    slice x1, local copies, waits for them, and re-layouts: 9.68 us -> 2.05 us  [body(): exchanged[2]]
    all_to_all x1, waiting for transfers between devices: 11.8 us -> 14.7 us  [stacked_exchange(): received = lax.all_to_all(jnp.stack(parts), name, 0, 0)]
  transfers between devices with their start and end apart: 6 -> 6, of which waited for: 5 -> 5; matrix products, arithmetic and copies ran while one was open for 29% -> 25% of each run, Pallas kernels for 0% -> 0%
where the time goes in v1:
time: 217 us; the launch traced here: 216 us
  waiting for transfers between devices  78.8 us (36%)
  matrix products  33 us (15%)
  local copies, waits for them, and re-layouts  31 us (14%)
  other arithmetic  27.2 us (13%)
  starting transfers between devices  15.5 us (7%)
  blocking collectives  15.1 us (7%)
  between operations  15 us (7%)
    reduce_scatter x1, waiting for transfers between devices, body(): lax.psum_scatter(partial_sum, 'dp', scatter_dimension=2, tiled=True)  49.9 us
    all_to_all x1, blocking collectives, body(): lax.all_to_all(input_grads, 'seq', split_axis=1, concat_axis=2, tiled=True)  15.1 us
    all_to_all x1, waiting for transfers between devices, stacked_exchange(): received = lax.all_to_all(jnp.stack(parts), name, 0, 0)  14.7 us
    add x4, other arithmetic, one_block(): return total + jnp.stack([part_first, part_second], axis=1)  12.7 us
    dot_general x4, matrix products, attend(): jnp.einsum(score_form, q_heads, k_heads, preferred_element_type=jnp.float32)  9.31 us
    dot_general x4, matrix products, attend(): jnp.einsum(mix_form, attention_weights, v_heads, preferred_element_type=j...  9.24 us
    all_to_all x1, waiting for transfers between devices, body(): lax.all_to_all(flat_temporal, 'seq', split_axis=1, concat_axis=0, tiled=T...  6.13 us
    dot_general x4, matrix products, one_block(): lax.dot_general(cols_first, error_first, (((0,), (0,)), ((), ())), prefer...  5.51 us
  transfers between devices with their start and end apart: 6, of which 5 were waited for; matrix products, arithmetic and copies ran while one was open for 25% of the time, Pallas kernels for 0%

profile of v1, /device:TPU:0, one launch (start us, length us, event | category | flops | bytes accessed | tf_op | source)
XLA Modules:
  0.0 215.8 jit_solution(14869628687250926888)
XLA Ops:
  7.9 1.3 fusion.57
  10.5 0.7 reduce.6
  11.3 2.0 fusion.13
  13.4 1.2 pad_maximum_fusion
  14.6 4.3 %all-to-all-start = ((bf16[4,4,1,32,1152]{4,3,1,2,0:T(8,128)(2,1)}), bf16[4,4,1,32,1152]{4,3,1,2,0:T(8,128)(2,1)}, u32[]{:S(2)}, u32[]{:S(2)}) async-start(bf16[4,4,1,32,1152]{4,3,1,2,0:T(8,128)(2,1)} %pad_maximum_fusion), calls=%async_computation | async-start | bytes 2359296 | tf_op jit(solution)/shard_map/all_to_all | solution.py:12
  18.9 1.2 fusion.56
  20.1 0.9 copy.101
  21.0 0.9 copy.100
  21.9 0.9 copy.102
  23.5 1.5 fusion.59
  25.0 1.3 fusion.17
  26.3 14.7 %all-to-all-done = bf16[4,4,1,32,1152]{4,3,1,2,0:T(8,128)(2,1)} async-done(((bf16[4,4,1,32,1152]{4,3,1,2,0:T(8,128)(2,1)}), bf16[4,4,1,32,1152]{4,3,1,2,0:T(8,128)(2,1)}, u32[]{:S(2)}, u32[]{:S(2)}) %all-to-all-start) | async-done | bytes 1179680 | tf_op jit(solution)/shard_map/all_to_all | solution.py:12
  41.0 2.0 fusion.55
  43.0 2.7 %reshape_squeeze.6 = bf16[4,32,16,72]{3,2,1,0:T(8,128)(2,1)} reshape(bf16[1,4,1,32,1152]{4,3,0,2,1:T(8,128)(2,1)} %get-tuple-element.317) | data formatting | bytes 589824 | tf_op jit(solution)/shard_map/jvp()/reshape;squeeze | solution.py:20
  45.8 1.7 reshape_squeeze.15
  47.5 1.8 reshape_squeeze.14
  49.3 0.9 reshape.200
  50.2 2.7 %fusion.58 = (f32[32,16,4]{2,1,0:T(8,128)S(1)}, f32[32,16,4,4]{2,3,1,0:T(4,128)S(1)}) fusion(bf16[4,32,16,72]{3,2,1,0:T(8,128)(2,1)} %reshape_squeeze.15, bf16[4,32,16,72]{3,2,1,0:T(8,128)(2,1)} %reshape_squeeze.14, pred[4]{0:T(512)(128)(4,1)S(1)} %iota_compare_fusion.1), kind=kOutput, calls=%fused_computation.102 | convolution fusion | flops 1202176 | bytes 630788 | tf_op jit(solution)/shard_map/jvp(qbhd,kbhd->bhqk)/dot_general | solution.py:21
  53.0 1.0 fusion.52
  54.0 3.9 %convert_reduce_fusion = (f32[32,16,4]{2,1,0:T(8,128)}, pred[32,16,4,4]{2,3,1,0:T(4,128)(4,1)}, f32[32,16,4]{2,1,0:T(8,128)S(1)}, bf16[32,16,4,4]{2,3,1,0:T(4,128)(2,1)S(1)}) fusion(f32[32,16,4,4]{2,3,1,0:T(4,128)S(1)} %get-tuple-element.333, f32[32,16,4]{2,1,0:T(8,128)S(1)} %get-tuple-element.332, f32[32,16,4]{2,1,0:T(8,128)S(1)} %multiply_divide_fusion, ...), kind=kOutput, calls=%fused_computation.58 | convolution fusion | flops 1249280 | bytes 679936 | tf_op jit(solution)/shard_map/transpose(jvp(bhqk,kbhd->qbhd))/dot_general | solution.py:28
  57.9 2.7 %fusion.53 = (f32[32,16,4]{2,1,0:T(8,128)}, f32[32,16,4,4]{2,3,1,0:T(4,128)}, bf16[32,16,4,4]{2,3,1,0:T(4,128)(2,1)S(1)}) fusion(f32[32,16,4,4]{2,3,1,0:T(4,128)S(1)} %get-tuple-element.333, f32[32,16,4]{2,1,0:T(8,128)S(1)} %get-tuple-element.332, f32[32,16,4]{2,1,0:T(8,128)S(1)} %neg.9, f32[32,16,4]{2,1,0:T(8,128)S(1)} %fusion.52, ...), kind=kLoop, calls=%fused_computation.98 | loop fusion | flops 63488 | bytes 131072 | tf_op jit(solution)/shard_map/transpose(jvp())/reduce_sum | solution.py:25
  60.6 0.8 fusion.21
  61.5 1.3 convert_element_type.190
  62.8 3.6 %all-to-all-start.3 = ((bf16[4,32,1152]{2,1,0:T(8,128)(2,1)}), bf16[4,32,1152]{2,1,0:T(8,128)(2,1)S(1)}, u32[]{:S(2)}, u32[]{:S(2)}) async-start(bf16[4,32,1152]{2,1,0:T(8,128)(2,1)} %convert_element_type.190), calls=%async_computation.3 | async-start | bytes 589824 | tf_op jit(solution)/shard_map/all_to_all | solution.py:74
  66.5 2.7 %convolution_convert_fusion.8 = bf16[16,128,72]{1,2,0:T(8,128)(2,1)} fusion(bf16[128,16,72]{0,2,1:T(8,128)(2,1)S(1)} %bitcast.112, f32[16,128]{1,0:T(8,128)S(1)} %fusion.59, f32[16,128,128]{1,2,0:T(8,128)} %fusion.17), kind=kOutput, calls=%fused_computation.47 | convolution fusion | flops 38684800 | bytes 1646592 | tf_op jit(solution)/shard_map/bhqk,bkhd->bqhd/dot_general | solution.py:28
  69.1 3.4 %all-to-all-done.3 = bf16[4,32,1152]{2,1,0:T(8,128)(2,1)S(1)} async-done(((bf16[4,32,1152]{2,1,0:T(8,128)(2,1)}), bf16[4,32,1152]{2,1,0:T(8,128)(2,1)S(1)}, u32[]{:S(2)}, u32[]{:S(2)}) %all-to-all-start.3) | async-done | bytes 294944 | tf_op jit(solution)/shard_map/all_to_all | solution.py:74
  72.6 0.7 copy-done.1
  73.3 3.5 %all-to-all-start.2 = ((bf16[128,4,288]{0,2,1:T(8,128)(2,1)}), bf16[128,4,288]{0,2,1:T(8,128)(2,1)S(1)}, u32[]{:S(2)}, u32[]{:S(2)}) async-start(bf16[128,4,288]{0,2,1:T(8,128)(2,1)} %bitcast.113), calls=%async_computation.2 | async-start | bytes 589824 | tf_op jit(solution)/shard_map/all_to_all | solution.py:81
  76.8 1.3 all_to_all.49
  78.1 1.0 copy.108
  79.1 4.0 %all-to-all-done.2 = bf16[128,4,288]{0,2,1:T(8,128)(2,1)S(1)} async-done(((bf16[128,4,288]{0,2,1:T(8,128)(2,1)}), bf16[128,4,288]{0,2,1:T(8,128)(2,1)S(1)}, u32[]{:S(2)}, u32[]{:S(2)}) %all-to-all-start.2) | async-done | bytes 294944 | tf_op jit(solution)/shard_map/all_to_all | solution.py:81
  83.1 4.1 %all-to-all-start.4 = ((bf16[128,4,288]{0,2,1:T(8,128)(2,1)}), bf16[128,4,288]{0,2,1:T(8,128)(2,1)}, u32[]{:S(2)}, u32[]{:S(2)}) async-start(bf16[128,4,288]{0,2,1:T(8,128)(2,1)} %copy.108), calls=%async_computation.4 | async-start | bytes 589824 | tf_op jit(solution)/shard_map/all_to_all | solution.py:82
  87.5 6.1 %all-to-all-done.4 = bf16[128,4,288]{0,2,1:T(8,128)(2,1)} async-done(((bf16[128,4,288]{0,2,1:T(8,128)(2,1)}), bf16[128,4,288]{0,2,1:T(8,128)(2,1)}, u32[]{:S(2)}, u32[]{:S(2)}) %all-to-all-start.4) | async-done | bytes 294944 | tf_op jit(solution)/shard_map/all_to_all | solution.py:82
  93.6 1.2 copy.116
  94.8 29.1 %while.16 = (s32[]{:T(128)}, f32[288,2,1152]{2,0,1:T(8,128)}, bf16[512,288]{1,0:T(8,128)(2,1)S(1)}, s32[]{:T(128)}, s32[]{:T(128)}, /*index=5*/bf16[512,1152]{1,...) while((s32[]{:T(128)}, f32[288,2,1152]{2,0,1:T(8,128)}, ...), condition=%wide.region_8.9_spmd.clone, body=%wide.region_7.8_spmd.clone.sunk | while | flops 174369792 | bytes 8787673 | solution.py:112
  94.9 1.3 and_convert_fusion.3
  96.2 1.4 fusion.76
  97.6 1.4 fusion.75
  99.0 1.9 select_add_fusion.2
  100.8 1.3 and_convert_fusion.3
  102.2 1.4 fusion.76
  103.6 1.4 fusion.75
  104.9 3.6 %select_add_fusion.2 = f32[288,2,1152]{2,0,1:T(8,128)} fusion(f32[288,2,1152]{2,0,1:T(8,128)} %get-tuple-element.407, bf16[288,1,1152]{2,0,1:T(8,128)(2,1)S(1)} %fusion.75, bf16[288,1,1152]{2,0,1:T(8,128)(2,1)S(1)} %fusion.76, pred[]{:T(512)S(6)} %compare.19), kind=kLoop, calls=%fused_computation.clone.1 | loop fusion | flops 2654208 | bytes 6635521 | tf_op jit(solution)/shard_map/while/body/eval_jaxpr/add | solution.py:110
  108.6 1.3 and_convert_fusion.3
  109.9 1.4 fusion.76
  111.3 1.4 fusion.75
  112.7 3.6 %select_add_fusion.2 = f32[288,2,1152]{2,0,1:T(8,128)} fusion(f32[288,2,1152]{2,0,1:T(8,128)} %get-tuple-element.407, bf16[288,1,1152]{2,0,1:T(8,128)(2,1)S(1)} %fusion.75, bf16[288,1,1152]{2,0,1:T(8,128)(2,1)S(1)} %fusion.76, pred[]{:T(512)S(6)} %compare.19), kind=kLoop, calls=%fused_computation.clone.1 | loop fusion | flops 2654208 | bytes 6635521 | tf_op jit(solution)/shard_map/while/body/eval_jaxpr/add | solution.py:110
  116.3 1.3 and_convert_fusion.3
  117.6 1.4 fusion.76
  119.0 1.4 fusion.75
  120.4 3.6 %select_add_fusion.2 = f32[288,2,1152]{2,0,1:T(8,128)} fusion(f32[288,2,1152]{2,0,1:T(8,128)} %get-tuple-element.407, bf16[288,1,1152]{2,0,1:T(8,128)(2,1)S(1)} %fusion.75, bf16[288,1,1152]{2,0,1:T(8,128)(2,1)S(1)} %fusion.76, pred[]{:T(512)S(6)} %compare.19), kind=kLoop, calls=%fused_computation.clone.1 | loop fusion | flops 2654208 | bytes 6635521 | tf_op jit(solution)/shard_map/while/body/eval_jaxpr/add | solution.py:110
  124.0 3.6 %copy.111 = f32[288,2,1152]{0,2,1:T(8,128)} copy(f32[288,2,1152]{2,0,1:T(8,128)} %get-tuple-element.226) | data formatting | bytes 5308416 | tf_op jit(solution)/shard_map/while | solution.py:112
  127.6 0.9 copy-done.4
  128.5 1.0 negate_divide_fusion
  129.6 2.6 %fusion.18 = bf16[4,32,16,72]{3,0,2,1:T(4,128)(2,1)S(1)} fusion(bf16[4,32,16,72]{3,2,1,0:T(8,128)(2,1)S(1)} %copy-done.7, f32[32,16,4,4]{2,3,1,0:T(4,128)} %get-tuple-element.312, pred[32,16,4,4]{2,3,1,0:T(4,128)(4,1)} %get-tuple-element.314, f32[32,16,4]{2,1,0:T(8,128)S(1)} %negate_divide_fusion, pred[4]{0:T(512)(128)(4,1)S(1)} %iota_compare_fusion.1), kind=kOutput, calls=%fused_computation.43 | convolution fusion | flops 1359872 | bytes 638980 | tf_op jit(solution)/shard_map/transpose(jvp(qbhd,kbhd->bhqk))/dot_general | solution.py:21
  132.8 2.6 %fusion.19 = bf16[4,32,16,72]{3,0,2,1:T(4,128)(2,1)S(1)} fusion(bf16[4,32,16,72]{3,2,1,0:T(8,128)(2,1)} %reshape_squeeze.14, f32[32,16,4,4]{2,3,1,0:T(4,128)} %get-tuple-element.312, pred[32,16,4,4]{2,3,1,0:T(4,128)(4,1)} %get-tuple-element.314, f32[32,16,4]{2,1,0:T(8,128)} %copy-done.11, pred[4]{0:T(512)(128)(4,1)S(1)} %iota_compare_fusion.1), kind=kOutput, calls=%fused_computation.44 | convolution fusion | flops 1359872 | bytes 638980 | tf_op jit(solution)/shard_map/transpose(jvp(qbhd,kbhd->bhqk))/dot_general | solution.py:21
  135.5 1.2 reshape.202
  136.8 1.9 fusion.20
  138.7 1.2 reshape.203
  140.0 1.2 pad_maximum_fusion.1
  141.2 15.1 %all_to_all.58 = bf16[3,4,32,1152]{3,2,0,1:T(8,128)(2,1)S(1)} all-to-all(bf16[3,4,32,1152]{3,2,0,1:T(8,128)(2,1)S(1)} %copy.98), channel_id=1, replica_groups=mesh['dp'=8,'seq'=4] {'seq'}, dimensions={1} | all-to-all | bytes 1769472 | tf_op jit(solution)/shard_map/all_to_all | solution.py:75
  156.3 1.0 copy.99
  157.3 49.9 %reduce-scatter.2.cloned.1.call-done = f32[288,2,144]{0,2,1:T(8,128)} async-done(((f32[288,2,1152]{0,2,1:T(8,128)}), f32[288,2,144]{0,2,1:T(8,128)}) %reduce-scatter.2.cloned.1.call-update) | async-done | bytes 331792 | tf_op jit(solution)/shard_map/reduce_scatter | solution.py:113
  207.2 1.8 slice_bitcast_fusion
  (52 shorter events, 3.6 us)
Async XLA Ops:
  7.2 4.1 %copy-start = (bf16[1152,1152]{1,0:T(8,128)(2,1)S(1)}, bf16[1152,1152]{1,0:T(8,128)(2,1)}, u32[]{:S(2)}) copy-start(bf16[1152,1152]{1,0:T(8,128)(2,1)} %param.14) | copy-start | bytes 7962628
  7.2 87.6 %all-gather.3.cloned.1.call-start = ((), (), s32[]{:S(2)}) async-start(), calls=%async_computation.7 | async-start | bytes 1474560 | tf_op jit(solution)/shard_map/all_gather | solution.py:87
  11.2 2.0 copy-start.5
  14.6 26.4 %all-to-all-start = ((bf16[4,4,1,32,1152]{4,3,1,2,0:T(8,128)(2,1)}), bf16[4,4,1,32,1152]{4,3,1,2,0:T(8,128)(2,1)}, u32[]{:S(2)}, u32[]{:S(2)}) async-start(bf16[4,4,1,32,1152]{4,3,1,2,0:T(8,128)(2,1)} %pad_maximum_fusion), calls=%async_computation | async-start | bytes 2359296 | tf_op jit(solution)/shard_map/all_to_all | solution.py:12
  21.0 2.5 %copy-start.2 = (bf16[1,1,1,128,1152]{3,4,2,1,0:T(8,128)(2,1)S(1)}, bf16[1,1,1,128,1152]{3,4,2,1,0:T(8,128)(2,1)}, u32[]{:S(2)}) copy-start(bf16[1,1,1,128,1152]{3,4,2,1,0:T(8,128)(2,1)} %copy.101) | copy-start | bytes 884740
  22.8 2.2 %copy-start.3 = (bf16[1,1,1,128,1152]{3,4,2,1,0:T(8,128)(2,1)S(1)}, bf16[1,1,1,128,1152]{3,4,2,1,0:T(8,128)(2,1)}, u32[]{:S(2)}) copy-start(bf16[1,1,1,128,1152]{3,4,2,1,0:T(8,128)(2,1)} %copy.100) | copy-start | bytes 884740
  50.2 3.8 %copy-start.6 = (bf16[4,32,16,72]{3,2,1,0:T(8,128)(2,1)}, bf16[4,32,16,72]{3,2,1,0:T(8,128)(2,1)S(1)}, u32[]{:S(2)}) copy-start(bf16[4,32,16,72]{3,2,1,0:T(8,128)(2,1)S(1)} %reshape.200) | copy-start | bytes 884740
  53.0 1.0 copy-start.8
  60.6 0.9 copy-start.9
  61.5 5.0 %copy-start.10 = (bf16[1,1,1,128,1152]{3,4,2,1,0:T(8,128)(2,1)S(1)}, bf16[1,1,1,128,1152]{3,4,2,1,0:T(8,128)(2,1)}, u32[]{:S(2)}) copy-start(bf16[1,1,1,128,1152]{3,4,2,1,0:T(8,128)(2,1)} %copy.102) | copy-start | bytes 884740
  62.8 9.8 %all-to-all-start.3 = ((bf16[4,32,1152]{2,1,0:T(8,128)(2,1)}), bf16[4,32,1152]{2,1,0:T(8,128)(2,1)S(1)}, u32[]{:S(2)}, u32[]{:S(2)}) async-start(bf16[4,32,1152]{2,1,0:T(8,128)(2,1)} %convert_element_type.190), calls=%async_computation.3 | async-start | bytes 589824 | tf_op jit(solution)/shard_map/all_to_all | solution.py:74
  72.6 0.7 copy-start.1
  73.3 9.8 %all-to-all-start.2 = ((bf16[128,4,288]{0,2,1:T(8,128)(2,1)}), bf16[128,4,288]{0,2,1:T(8,128)(2,1)S(1)}, u32[]{:S(2)}, u32[]{:S(2)}) async-start(bf16[128,4,288]{0,2,1:T(8,128)(2,1)} %bitcast.113), calls=%async_computation.2 | async-start | bytes 589824 | tf_op jit(solution)/shard_map/all_to_all | solution.py:81
  78.1 16.7 %copy-start.12 = (f32[1,1152]{1,0:T(1,128)S(1)}, f32[1,1152]{1,0:T(1,128)}, u32[]{:S(2)}) copy-start(f32[1,1152]{1,0:T(1,128)} %param.13) | copy-start | bytes 13828
  78.1 16.7 %copy-start.13 = (f32[1,1152]{1,0:T(1,128)S(1)}, f32[1,1152]{1,0:T(1,128)}, u32[]{:S(2)}) copy-start(f32[1,1152]{1,0:T(1,128)} %param.12) | copy-start | bytes 13828
  83.1 10.5 %all-to-all-start.4 = ((bf16[128,4,288]{0,2,1:T(8,128)(2,1)}), bf16[128,4,288]{0,2,1:T(8,128)(2,1)}, u32[]{:S(2)}, u32[]{:S(2)}) async-start(bf16[128,4,288]{0,2,1:T(8,128)(2,1)} %copy.108), calls=%async_computation.4 | async-start | bytes 589824 | tf_op jit(solution)/shard_map/all_to_all | solution.py:82
  87.2 120.0 %reduce-scatter.2.cloned.1.call-start = ((), (), s32[]{:S(2)}) async-start(), calls=%async_computation.6 | async-start | bytes 3981312 | tf_op jit(solution)/shard_map/reduce_scatter | solution.py:113
  127.6 0.9 copy-start.4
  127.6 2.0 copy-start.7
  129.5 2.7 %copy-start.11 = (f32[32,16,4]{2,1,0:T(8,128)}, f32[32,16,4]{2,1,0:T(8,128)S(1)}, u32[]{:S(2)}) copy-start(f32[32,16,4]{2,1,0:T(8,128)S(1)} %negate_divide_fusion) | copy-start | bytes 24580
Sparse Core Ops, SparseCore 0:
  9.5 25.8 all-gather.2
  127.7 79.3 reduce-scatter.1
